TPU v7x, 128 devices: a whole 4x4x4 slice. The times are simulated.
128 devices in a mesh: wide: 16 (over z_hi, y, core), narrow: 8 (over x, z_lo).
Axes of the slice: x: 4, y: 4, z: 4 (z_hi: 2, z_lo: 2; z = z_hi * 2 + z_lo), core: 2. Of those that a mesh axis runs over, the one named last changes fastest.
Arguments:
- field: float32 [4, 512, 512, 256], P(None, 'wide', 'narrow'), may hold values from -70 to 70, as said below
- start_first: float32 [512, 128], replicated, may hold values from -5 to 5
- start_second: float32 [512, 128], replicated, may hold values from -5 to 5
Outputs:
- core_tensor: float32 [256, 4, 128, 128], P('wide', None, 'narrow')
- basis_first: float32 [512, 128], replicated
- basis_second: float32 [512, 128], replicated
Inputs may be any that keep to these rules, and one draw needn't show every extreme that they name: `field`: species fields with amplitudes that vary over mode 1, mode 2 and mode 3.
All inputs are finite; a program needn't handle non-finite values.
Results may differ from a plain program's by a relative error of at most 0.0003.
Values sent between devices are 32-bit elements; how exact they have to be, the bound alone decides.
No kernel may reach another device: no remote copies, remote signals or barrier semaphores. Data moves between devices by JAX's collectives and lax.ppermute only.
A program may use at most 192 MiB of HBM per device.

v0:
```python
import jax
import jax.numpy as jnp
from jax import lax
from jax.sharding import PartitionSpec as P

ITERS = 3


def split_up(x, dim, devices):
    before, after = (x.shape[:dim], x.shape[dim + 1 :])
    return jnp.moveaxis(x.reshape(*before, devices, -1, *after), dim, 0)


def summed_on_arrival(x, axis, dim):
    devices = lax.axis_size(axis)
    blocks = lax.all_to_all(split_up(x, dim, devices), axis, 0, 0, tiled=True)
    return jnp.sum(blocks, axis=0)


def copy_for_each(x, axis):
    devices = lax.axis_size(axis)
    return lax.all_to_all(jnp.broadcast_to(x[None], (devices, *x.shape)), axis, 0, 0, tiled=True)


def over_copies(x, axis):
    return copy_for_each(x, axis).sum(axis=0)


def in_order(blocks, dim):
    dims = list(blocks.shape[1:])
    dims[dim] *= blocks.shape[0]
    return jnp.moveaxis(blocks, 0, dim).reshape(dims)


def gathered_copies(x, axis, dim):
    return in_order(copy_for_each(x, axis), dim)


def items_in_groups(x, axis, split_dim, concat_dim, work, item_dim, out_dim):
    items = jax.tree.leaves(x)[0].shape[item_dim]
    count = 2 if items % 2 == 0 else 1
    done = []
    for k in range(count):
        group = jax.tree.map(
            lambda a: lax.slice_in_dim(
                a, k * (items // count), (k + 1) * (items // count), axis=item_dim
            ),
            x,
        )
        done.append(
            work(
                lax.all_to_all(
                    group, axis, split_axis=split_dim, concat_axis=concat_dim, tiled=True
                )
            )
        )
    return jax.tree.map(lambda *parts: jnp.concatenate(parts, axis=out_dim), *done)


def orthonormal(columns):
    gram_matrix = jnp.dot(columns.T, columns, precision=lax.Precision.HIGHEST)
    lower_factor = jnp.linalg.cholesky(gram_matrix)
    return jax.scipy.linalg.solve_triangular(lower_factor, columns.T, lower=True).T


def iterate_basis(upper, start):
    basis_now = orthonormal(start)
    for sweep in range(ITERS):
        inner = jnp.dot(upper, basis_now, precision=lax.Precision.HIGHEST)
        basis_now = orthonormal(jnp.dot(upper.T, inner, precision=lax.Precision.HIGHEST))
    return basis_now


def first_local(pencil_block):
    merged = pencil_block.reshape(
        pencil_block.shape[0], pencil_block.shape[1], pencil_block.shape[2] * pencil_block.shape[3]
    )
    partial_grams = jnp.einsum("siq,sjq->sij", merged, merged, precision=lax.Precision.HIGHEST)
    return (partial_grams, merged)


def second_local(slab_block):
    partial_grams = jnp.einsum(
        "srpt,srqt->spq", slab_block, slab_block, precision=lax.Precision.HIGHEST
    )
    return (partial_grams, slab_block)


def reduce_first(local_first):
    rows_first = summed_on_arrival(local_first, "narrow", 0)
    rows_first = over_copies(rows_first, "wide")
    return gathered_copies(rows_first, "narrow", 0)


def reduce_second(local_second):
    rows_second = summed_on_arrival(local_second, "narrow", 0)
    rows_second = over_copies(rows_second, "wide")
    return gathered_copies(rows_second, "narrow", 0)


def local(field, start_first, start_second):
    grams_first, pencil = items_in_groups(field, "wide", 3, 1, first_local, 0, 0)
    summed_first = reduce_first(jnp.sum(grams_first, axis=0))
    factor_first = jnp.linalg.cholesky(summed_first).T
    basis_first = iterate_basis(factor_first, start_first)
    reduced = jnp.einsum("ir,siq->srq", basis_first, pencil, precision=lax.Precision.HIGHEST)
    planes = field.shape[3] // lax.axis_size("wide")
    reduced = reduced.reshape(reduced.shape[0], reduced.shape[1], field.shape[2], planes)
    grams_second, slab = second_local(
        lax.all_to_all(reduced, "narrow", split_axis=1, concat_axis=2, tiled=True)
    )
    summed_second = reduce_second(jnp.sum(grams_second, axis=0))
    factor_second = jnp.linalg.cholesky(summed_second).T
    basis_second = iterate_basis(factor_second, start_second)
    core_tensor = jnp.einsum("pq,srpt->tsrq", basis_second, slab, precision=lax.Precision.HIGHEST)
    return (core_tensor, basis_first, basis_second)


def solution(mesh):
    placed = (P(None, "wide", "narrow", None), P(), P())
    return jax.shard_map(
        local,
        mesh=mesh,
        in_specs=placed,
        out_specs=(P("wide", None, "narrow", None), P(), P()),
        check_vma=False,
    )
```

profile of v0, /device:TPU:1, one launch (start us, length us, event | category | flops | bytes accessed | tf_op | source)
XLA Modules:
  0.0 857.5 jit_solution(4659479171847985176)
XLA Ops:
  0.6 7.9 fusion.150
  8.5 9.1 %copy.145 = f32[2,32,64,256]{2,1,0,3:T(8,128)} copy(f32[2,32,64,256]{3,2,1,0:T(8,128)} %get-tuple-element.22) | data formatting | bytes 8388608
  17.7 13.3 %reshape.79 = f32[16,1,65536]{2,1,0:T(1,128)} reshape(f32[256,2,32,64]{3,2,1,0:T(8,128)} %bitcast.260) | data formatting | bytes 8388608
  31.0 9.3 %all-to-all-start.1 = ((f32[16,1,65536]{2,1,0:T(1,128)}), f32[16,1,65536]{2,1,0:T(1,128)}, u32[]{:S(2)}, u32[]{:S(2)}) async-start(f32[16,1,65536]{2,1,0:T(1,128)} %reshape.79), calls=%async_computation.1 | async-start | bytes 8388608 | tf_op jit(solution)/shard_map/all_to_all | solution.py:52
  40.2 9.2 %copy.144 = f32[2,32,64,256]{2,1,0,3:T(8,128)} copy(f32[2,32,64,256]{3,2,1,0:T(8,128)} %get-tuple-element.21) | data formatting | bytes 8388608
  49.4 13.3 %reshape.81 = f32[16,1,65536]{2,1,0:T(1,128)} reshape(f32[256,2,32,64]{3,2,1,0:T(8,128)} %bitcast.261) | data formatting | bytes 8388608
  62.7 33.4 %all-to-all-done.1 = f32[16,1,65536]{2,1,0:T(1,128)} async-done(((f32[16,1,65536]{2,1,0:T(1,128)}), f32[16,1,65536]{2,1,0:T(1,128)}, u32[]{:S(2)}, u32[]{:S(2)}) %all-to-all-start.1) | async-done | bytes 4194336 | tf_op jit(solution)/shard_map/all_to_all | solution.py:52
  96.1 7.0 all-to-all-start
  103.6 13.7 %reduce.22 = f32[16,65536]{1,0:T(8,128)} reduce(f32[16,1,65536]{2,1,0:T(1,128)} %all-to-all-done.1, f32[]{:T(128)} %broadcast.156), dimensions={1}, to_apply=%all_to_all.56.reduce_sub_computation | reduce | bytes 8388612 | tf_op jit(solution)/shard_map/all_to_all | solution.py:52
  117.3 6.9 reshape.80
  124.2 16.3 %copy.110 = f32[2,16,32,64,16]{2,1,4,3,0:T(8,128)} copy(f32[2,16,32,64,16]{3,2,0,4,1:T(8,128)} %bitcast.258) | data formatting | bytes 8388608 | tf_op jit(solution)/shard_map/all_to_all | solution.py:52
  140.5 12.9 %reshape.66 = f32[2,512,1024]{1,2,0:T(8,128)} reshape(f32[2,16,32,64,16]{2,1,4,3,0:T(8,128)} %copy.110) | data formatting | bytes 8388608 | tf_op jit(solution)/shard_map/reshape | solution.py:75
  153.4 5.3 all-to-all-done
  158.7 13.7 %reduce.23 = f32[16,65536]{1,0:T(8,128)} reduce(f32[16,1,65536]{2,1,0:T(1,128)} %all-to-all-done, f32[]{:T(128)} %broadcast.156), dimensions={1}, to_apply=%all_to_all.53.reduce_sub_computation | reduce | bytes 8388612 | tf_op jit(solution)/shard_map/all_to_all | solution.py:52
  172.4 6.9 reshape.82
  179.3 16.3 %copy.107 = f32[2,16,32,64,16]{2,1,4,3,0:T(8,128)} copy(f32[2,16,32,64,16]{3,2,0,4,1:T(8,128)} %bitcast.259) | data formatting | bytes 8388608 | tf_op jit(solution)/shard_map/all_to_all | solution.py:52
  195.6 12.9 %reshape.65 = f32[2,512,1024]{1,2,0:T(8,128)} reshape(f32[2,16,32,64,16]{2,1,4,3,0:T(8,128)} %copy.107) | data formatting | bytes 8388608 | tf_op jit(solution)/shard_map/reshape | solution.py:75
  208.6 5.4 copy.111
  214.0 9.4 %fusion.15 = f32[8,64,512]{2,1,0:T(8,128)S(1)} fusion(f32[8,64,1024,2]{2,1,0,3:T(8,128)} %bitcast.266, f32[2,512,1024]{1,2,0:T(8,128)} %reshape.65), kind=kOutput, calls=%fused_computation.13 | convolution fusion | flops 6442450944 | bytes 9437184 | tf_op jit(solution)/shard_map/siq,sjq->sij/dot_general | solution.py:78
  223.4 5.4 copy.113
  228.8 9.5 %fusion.21 = f32[8,64,512]{2,1,0:T(8,128)S(1)} fusion(f32[8,64,512]{2,1,0:T(8,128)S(1)} %fusion.15, f32[8,64,1024,2]{2,1,0,3:T(8,128)} %bitcast.264, f32[2,512,1024]{1,2,0:T(8,128)} %reshape.66), kind=kOutput, calls=%fused_computation.15 | convolution fusion | flops 6442713088 | bytes 10485760 | tf_op jit(solution)/shard_map/siq,sjq->sij/dot_general | solution.py:78
  238.3 18.6 %all_to_all.78 = f32[8,64,512]{2,1,0:T(8,128)S(1)} all-to-all(f32[8,64,512]{2,1,0:T(8,128)S(1)} %fusion.21), channel_id=1, replica_groups=mesh['wide'=16,'narrow'=8] {'narrow'}, dimensions={0} | all-to-all | bytes 2097152 | tf_op jit(solution)/shard_map/all_to_all | solution.py:16
  258.5 8.2 all-to-all-start.3
  267.4 27.8 %all-to-all-done.3 = f32[16,64,512]{2,1,0:T(8,128)S(1)} async-done(((f32[16,64,512]{2,1,0:T(8,128)}), f32[16,64,512]{2,1,0:T(8,128)S(1)}, u32[]{:S(2)}, u32[]{:S(2)}) %all-to-all-start.3) | async-done | bytes 2097184 | tf_op jit(solution)/shard_map/all_to_all | solution.py:22
  300.3 11.7 %cholesky.488 = f32[128,128]{1,0:T(8,128)S(1)} custom-call(f32[128,128]{1,0:T(8,128)S(1)} %fusion.101), custom_call_target="Cholesky" | custom-call | tf_op jit(solution)/shard_map/jit(cholesky)/cholesky | solution.py:62
  313.4 9.8 %custom-call.38 = f32[1,128,128]{1,2,0:T(8,128)S(1)} custom-call(f32[1,128,128]{2,1,0:T(8,128)S(1)} %fusion.71), custom_call_target="InvertDiagBlocksLowerTriangular" | custom-call | tf_op jit(solution)/shard_map/jit(_solve_triangular)/triangular_solve | solution.py:63
  324.9 11.7 %cholesky.418 = f32[128,128]{1,0:T(8,128)S(1)} custom-call(f32[128,128]{1,0:T(8,128)S(1)} %cholesky.646), custom_call_target="Cholesky" | custom-call | tf_op jit(solution)/shard_map/jit(cholesky)/cholesky | solution.py:104
  336.8 10.2 %custom-call.35 = f32[1,128,128]{1,2,0:T(8,128)S(1)} custom-call(f32[1,128,128]{2,1,0:T(8,128)S(1)} %get-tuple-element.42), custom_call_target="InvertDiagBlocksLowerTriangular" | custom-call | tf_op jit(solution)/shard_map/jit(cholesky)/cholesky | solution.py:104
  347.7 11.7 %cholesky.437 = f32[128,128]{1,0:T(8,128)S(1)} custom-call(f32[128,128]{1,0:T(8,128)S(1)} %cholesky.650), custom_call_target="Cholesky" | custom-call | tf_op jit(solution)/shard_map/jit(cholesky)/cholesky | solution.py:104
  359.4 9.8 %custom-call.36 = f32[1,128,128]{1,2,0:T(8,128)S(1)} custom-call(f32[1,128,128]{2,1,0:T(8,128)S(1)} %get-tuple-element.39), custom_call_target="InvertDiagBlocksLowerTriangular" | custom-call | tf_op jit(solution)/shard_map/jit(cholesky)/cholesky | solution.py:104
  369.9 11.7 %cholesky.458 = f32[128,128]{1,0:T(8,128)S(1)} custom-call(f32[128,128]{1,0:T(8,128)S(1)} %cholesky.655), custom_call_target="Cholesky" | custom-call | tf_op jit(solution)/shard_map/jit(cholesky)/cholesky | solution.py:104
  381.7 10.0 %custom-call.37 = f32[1,128,128]{1,2,0:T(8,128)S(1)} custom-call(f32[1,128,128]{2,1,0:T(8,128)S(1)} %get-tuple-element.36), custom_call_target="InvertDiagBlocksLowerTriangular" | custom-call | tf_op jit(solution)/shard_map/jit(cholesky)/cholesky | solution.py:104
  392.2 11.7 %cholesky.475 = f32[128,128]{1,0:T(8,128)S(1)} custom-call(f32[128,128]{1,0:T(8,128)S(1)} %convolution_subtract_fusion.5), custom_call_target="Cholesky" | custom-call | tf_op jit(solution)/shard_map/jit(cholesky)/cholesky | solution.py:104
  411.3 12.1 %cholesky.499 = f32[128,128]{1,0:T(8,128)S(1)} custom-call(f32[128,128]{1,0:T(8,128)S(1)} %fusion.99), custom_call_target="Cholesky" | custom-call | tf_op jit(solution)/shard_map/jit(cholesky)/cholesky | solution.py:62
  424.7 9.8 %custom-call.39 = f32[1,128,128]{1,2,0:T(8,128)S(1)} custom-call(f32[1,128,128]{2,1,0:T(8,128)S(1)} %fusion.72), custom_call_target="InvertDiagBlocksLowerTriangular" | custom-call | tf_op jit(solution)/shard_map/jit(_solve_triangular)/triangular_solve | solution.py:63
  437.9 11.7 %cholesky.510 = f32[128,128]{1,0:T(8,128)S(1)} custom-call(f32[128,128]{1,0:T(8,128)S(1)} %fusion.97), custom_call_target="Cholesky" | custom-call | tf_op jit(solution)/shard_map/jit(cholesky)/cholesky | solution.py:62
  450.9 10.0 %custom-call.40 = f32[1,128,128]{1,2,0:T(8,128)S(1)} custom-call(f32[1,128,128]{2,1,0:T(8,128)S(1)} %fusion.73), custom_call_target="InvertDiagBlocksLowerTriangular" | custom-call | tf_op jit(solution)/shard_map/jit(_solve_triangular)/triangular_solve | solution.py:63
  464.2 11.7 %cholesky.521 = f32[128,128]{1,0:T(8,128)S(1)} custom-call(f32[128,128]{1,0:T(8,128)S(1)} %fusion.95), custom_call_target="Cholesky" | custom-call | tf_op jit(solution)/shard_map/jit(cholesky)/cholesky | solution.py:62
  477.3 9.8 %custom-call.41 = f32[1,128,128]{1,2,0:T(8,128)S(1)} custom-call(f32[1,128,128]{2,1,0:T(8,128)S(1)} %fusion.74), custom_call_target="InvertDiagBlocksLowerTriangular" | custom-call | tf_op jit(solution)/shard_map/jit(_solve_triangular)/triangular_solve | solution.py:63
  487.6 9.2 %fusion = f32[4,1024,128]{2,1,0:T(8,128)S(1)} fusion(f32[2,512,1024]{1,2,0:T(8,128)} %reshape.66, f32[2,512,1024]{1,2,0:T(8,128)} %reshape.65, f32[128,512]{1,0:T(8,128)S(1)} %fusion.41), kind=kOutput, calls=%fused_computation | convolution fusion | flops 3223322624 | bytes 10747904 | tf_op jit(solution)/shard_map/ir,siq->srq/dot_general | solution.py:106
  501.3 5.9 reshape.83
  507.3 30.3 %all_to_all.79 = f32[8,1,65536]{2,1,0:T(1,128)} all-to-all(f32[8,1,65536]{2,1,0:T(1,128)S(1)} %reshape.83), channel_id=1, replica_groups=mesh['wide'=16,'narrow'=8] {'narrow'}, dimensions={0} | all-to-all | bytes 4194304 | tf_op jit(solution)/shard_map/all_to_all | solution.py:110
  537.6 7.2 reduce.24
  548.4 7.4 copy.122
  559.3 4.8 reshape.75
  566.8 10.4 %fusion.12 = f32[8,64,512]{2,1,0:T(8,128)S(1)} fusion(f32[4,16,512,16,1]{2,3,0,1,4:T(8,128)} %reshape.75, f32[8,64,16,16,4]{1,0,3,4,2:T(8,128)} %dot_general.105), kind=kOutput, calls=%fused_computation.12 | convolution fusion | flops 3221225472 | bytes 5242880 | tf_op jit(solution)/shard_map/srpt,srqt->spq/dot_general | solution.py:83
  577.2 15.6 %all_to_all.80 = f32[8,64,512]{2,1,0:T(8,128)S(1)} all-to-all(f32[8,64,512]{2,1,0:T(8,128)S(1)} %fusion.12), channel_id=1, replica_groups=mesh['wide'=16,'narrow'=8] {'narrow'}, dimensions={0} | all-to-all | bytes 2097152 | tf_op jit(solution)/shard_map/all_to_all | solution.py:16
  594.4 9.1 %all-to-all-start.7 = ((f32[16,64,512]{2,1,0:T(8,128)}), f32[16,64,512]{2,1,0:T(8,128)}, u32[]{:S(2)}, u32[]{:S(2)}) async-start(f32[16,64,512]{2,1,0:T(8,128)} %broadcast_in_dim.12), calls=%async_computation.7 | async-start | bytes 4194304 | tf_op jit(solution)/shard_map/all_to_all | solution.py:22
  604.3 27.9 %all-to-all-done.7 = f32[16,64,512]{2,1,0:T(8,128)} async-done(((f32[16,64,512]{2,1,0:T(8,128)}), f32[16,64,512]{2,1,0:T(8,128)}, u32[]{:S(2)}, u32[]{:S(2)}) %all-to-all-start.7) | async-done | bytes 2097184 | tf_op jit(solution)/shard_map/all_to_all | solution.py:22
  639.4 12.5 %cholesky.604 = f32[128,128]{1,0:T(8,128)S(1)} custom-call(f32[128,128]{1,0:T(8,128)} %fusion.90), custom_call_target="Cholesky" | custom-call | tf_op jit(solution)/shard_map/jit(cholesky)/cholesky | solution.py:62
  653.3 9.8 %custom-call.45 = f32[1,128,128]{1,2,0:T(8,128)S(1)} custom-call(f32[1,128,128]{2,1,0:T(8,128)S(1)} %fusion.75), custom_call_target="InvertDiagBlocksLowerTriangular" | custom-call | tf_op jit(solution)/shard_map/jit(_solve_triangular)/triangular_solve | solution.py:63
  670.7 11.7 %cholesky.534 = f32[128,128]{1,0:T(8,128)S(1)} custom-call(f32[128,128]{1,0:T(8,128)S(1)} %cholesky.659), custom_call_target="Cholesky" | custom-call | tf_op jit(solution)/shard_map/jit(cholesky)/cholesky | solution.py:113
  682.6 10.0 %custom-call.42 = f32[1,128,128]{1,2,0:T(8,128)S(1)} custom-call(f32[1,128,128]{2,1,0:T(8,128)S(1)} %get-tuple-element.32), custom_call_target="InvertDiagBlocksLowerTriangular" | custom-call | tf_op jit(solution)/shard_map/jit(cholesky)/cholesky | solution.py:113
  695.8 11.7 %cholesky.553 = f32[128,128]{1,0:T(8,128)S(1)} custom-call(f32[128,128]{1,0:T(8,128)S(1)} %cholesky.663), custom_call_target="Cholesky" | custom-call | tf_op jit(solution)/shard_map/jit(cholesky)/cholesky | solution.py:113
  707.5 9.8 %custom-call.43 = f32[1,128,128]{1,2,0:T(8,128)S(1)} custom-call(f32[1,128,128]{2,1,0:T(8,128)S(1)} %get-tuple-element.29), custom_call_target="InvertDiagBlocksLowerTriangular" | custom-call | tf_op jit(solution)/shard_map/jit(cholesky)/cholesky | solution.py:113
  720.4 13.2 %cholesky.574 = f32[128,128]{1,0:T(8,128)} custom-call(f32[128,128]{1,0:T(8,128)} %cholesky.668), custom_call_target="Cholesky" | custom-call | tf_op jit(solution)/shard_map/jit(cholesky)/cholesky | solution.py:113
  735.1 11.6 %custom-call.44 = f32[1,128,128]{1,2,0:T(8,128)} custom-call(f32[1,128,128]{2,1,0:T(8,128)} %get-tuple-element.26), custom_call_target="InvertDiagBlocksLowerTriangular" | custom-call | tf_op jit(solution)/shard_map/jit(cholesky)/cholesky | solution.py:113
  749.0 11.7 %cholesky.591 = f32[128,128]{1,0:T(8,128)S(1)} custom-call(f32[128,128]{1,0:T(8,128)S(1)} %convolution_subtract_fusion.4), custom_call_target="Cholesky" | custom-call | tf_op jit(solution)/shard_map/jit(cholesky)/cholesky | solution.py:113
  771.1 12.7 %cholesky.615 = f32[128,128]{1,0:T(8,128)S(1)} custom-call(f32[128,128]{1,0:T(8,128)} %fusion.88), custom_call_target="Cholesky" | custom-call | tf_op jit(solution)/shard_map/jit(cholesky)/cholesky | solution.py:62
  785.1 9.8 %custom-call.46 = f32[1,128,128]{1,2,0:T(8,128)S(1)} custom-call(f32[1,128,128]{2,1,0:T(8,128)S(1)} %fusion.76), custom_call_target="InvertDiagBlocksLowerTriangular" | custom-call | tf_op jit(solution)/shard_map/jit(_solve_triangular)/triangular_solve | solution.py:63
  800.6 12.5 %cholesky.626 = f32[128,128]{1,0:T(8,128)S(1)} custom-call(f32[128,128]{1,0:T(8,128)} %fusion.86), custom_call_target="Cholesky" | custom-call | tf_op jit(solution)/shard_map/jit(cholesky)/cholesky | solution.py:62
  814.5 10.0 %custom-call.47 = f32[1,128,128]{1,2,0:T(8,128)S(1)} custom-call(f32[1,128,128]{2,1,0:T(8,128)S(1)} %fusion.77), custom_call_target="InvertDiagBlocksLowerTriangular" | custom-call | tf_op jit(solution)/shard_map/jit(_solve_triangular)/triangular_solve | solution.py:63
  829.5 11.7 %cholesky.637 = f32[128,128]{1,0:T(8,128)S(1)} custom-call(f32[128,128]{1,0:T(8,128)S(1)} %fusion.84), custom_call_target="Cholesky" | custom-call | tf_op jit(solution)/shard_map/jit(cholesky)/cholesky | solution.py:62
  842.5 9.8 %custom-call.48 = f32[1,128,128]{1,2,0:T(8,128)S(1)} custom-call(f32[1,128,128]{2,1,0:T(8,128)S(1)} %fusion.78), custom_call_target="InvertDiagBlocksLowerTriangular" | custom-call | tf_op jit(solution)/shard_map/jit(_solve_triangular)/triangular_solve | solution.py:63
  (146 shorter events, 99.3 us)
Async XLA Ops:
  0.6 266.1 %copy-start = (f32[512,128]{1,0:T(8,128)S(1)}, f32[512,128]{1,0:T(8,128)}, u32[]{:S(2)}) copy-start(f32[512,128]{1,0:T(8,128)} %param.8) | copy-start | bytes 786436
  31.0 65.1 %all-to-all-start.1 = ((f32[16,1,65536]{2,1,0:T(1,128)}), f32[16,1,65536]{2,1,0:T(1,128)}, u32[]{:S(2)}, u32[]{:S(2)}) async-start(f32[16,1,65536]{2,1,0:T(1,128)} %reshape.79), calls=%async_computation.1 | async-start | bytes 8388608 | tf_op jit(solution)/shard_map/all_to_all | solution.py:52
  96.1 62.7 %all-to-all-start = ((f32[16,1,65536]{2,1,0:T(1,128)}), f32[16,1,65536]{2,1,0:T(1,128)}, u32[]{:S(2)}, u32[]{:S(2)}) async-start(f32[16,1,65536]{2,1,0:T(1,128)} %reshape.81), calls=%async_computation | async-start | bytes 8388608 | tf_op jit(solution)/shard_map/all_to_all | solution.py:52
  258.5 36.7 %all-to-all-start.3 = ((f32[16,64,512]{2,1,0:T(8,128)}), f32[16,64,512]{2,1,0:T(8,128)S(1)}, u32[]{:S(2)}, u32[]{:S(2)}) async-start(f32[16,64,512]{2,1,0:T(8,128)} %broadcast_in_dim.8), calls=%async_computation.3 | async-start | bytes 4194304 | tf_op jit(solution)/shard_map/all_to_all | solution.py:22
  296.5 27.8 %all-to-all-start.4 = ((f32[8,64,512]{2,1,0:T(8,128)}), f32[8,64,512]{2,1,0:T(8,128)S(1)}, u32[]{:S(2)}, u32[]{:S(2)}) async-start(f32[8,64,512]{2,1,0:T(8,128)} %broadcast_in_dim.10), calls=%async_computation.4 | async-start | bytes 2097152 | tf_op jit(solution)/shard_map/all_to_all | solution.py:22
  324.9 83.5 %copy-start.7 = (f32[128,512]{1,0:T(8,128)S(1)}, f32[128,512]{1,0:T(8,128)}, u32[]{:S(2)}) copy-start(f32[128,512]{1,0:T(8,128)} %fusion.47) | copy-start | bytes 786436
  487.5 9.3 %copy-start.6 = (f32[128,512]{1,0:T(8,128)}, f32[128,512]{1,0:T(8,128)S(1)}, u32[]{:S(2)}) copy-start(f32[128,512]{1,0:T(8,128)S(1)} %fusion.41) | copy-start | bytes 786436
  592.9 10.7 %copy-start.5 = (f32[512,128]{1,0:T(8,128)S(1)}, f32[512,128]{1,0:T(8,128)}, u32[]{:S(2)}) copy-start(f32[512,128]{1,0:T(8,128)} %param.9) | copy-start | bytes 786436
  594.4 37.7 %all-to-all-start.7 = ((f32[16,64,512]{2,1,0:T(8,128)}), f32[16,64,512]{2,1,0:T(8,128)}, u32[]{:S(2)}, u32[]{:S(2)}) async-start(f32[16,64,512]{2,1,0:T(8,128)} %broadcast_in_dim.12), calls=%async_computation.7 | async-start | bytes 4194304 | tf_op jit(solution)/shard_map/all_to_all | solution.py:22
  635.0 32.0 %all-to-all-start.8 = ((f32[8,64,512]{2,1,0:T(8,128)}), f32[8,64,512]{2,1,0:T(8,128)S(1)}, u32[]{:S(2)}, u32[]{:S(2)}) async-start(f32[8,64,512]{2,1,0:T(8,128)} %broadcast_in_dim.13), calls=%async_computation.8 | async-start | bytes 2097152 | tf_op jit(solution)/shard_map/all_to_all | solution.py:22
  669.7 1.0 copy-start.4
  695.1 0.7 copy-start.8
  769.1 0.7 copy-start.2
  798.5 0.7 copy-start.3
  828.1 0.7 copy-start.1
where the time goes:
time: 865 us; the launch traced here: 858 us
  other arithmetic  389 us (45%)
  local copies, waits for them, and re-layouts  185 us (21%)
  waiting for transfers between devices  94.5 us (11%)
  matrix products  76.9 us (9%)
  blocking collectives  64.5 us (7%)
  starting transfers between devices  41.1 us (5%)
    another operation x24, other arithmetic, orthonormal(): lower_factor = jnp.linalg.cholesky(gram_matrix)  102 us
    another operation x16, other arithmetic, orthonormal(): jax.scipy.linalg.solve_triangular(lower_factor, columns.T, lower=True)  84.1 us
    another operation x15, other arithmetic, local(): factor_second = jnp.linalg.cholesky(summed_second).T  84 us
    another operation x14, other arithmetic, local(): factor_first = jnp.linalg.cholesky(summed_first).T  78.9 us
    unnamed x29, local copies, waits for them, and re-layouts  75.5 us
    all_to_all x4, waiting for transfers between devices, copy_for_each(): lax.all_to_all(jnp.broadcast_to(x[None], (devices, *x.shape)), axis, 0, 0...  55.7 us
    all_to_all x2, waiting for transfers between devices, items_in_groups(): lax.all_to_all(group, axis, split_axis=split_dim, concat_axis=concat_dim,...  38.8 us
    all_to_all x2, blocking collectives, summed_on_arrival(): blocks = lax.all_to_all(split_up(x, dim, devices), axis, 0, 0, tiled=True)  34.2 us
  transfers between devices with their start and end apart: 6, of which 4 were waited for; matrix products, arithmetic and copies ran while one was open for 15% of the time, Pallas kernels for 0%

commit v1 on v0

v1 whole, which is shorter than its diff:
```python
import functools
import jax
import jax.numpy as jnp
from jax import lax
from jax.experimental import pallas as pl
from jax.experimental.pallas import tpu as pltpu
from jax.sharding import PartitionSpec as P

ITERS = 3
F32 = jnp.float32
BF16 = jnp.bfloat16
EXACT = lax.Precision.HIGHEST
ALL = ("wide", "narrow")
VMEM_LIMIT = 60 * 1024 * 1024

NN = (((1,), (0,)), ((), ()))
NT = (((1,), (1,)), ((), ()))
TN = (((0,), (0,)), ((), ()))


def dot32(a, b, dims):
    return lax.dot_general(a, b, dims, precision=EXACT, preferred_element_type=F32)


def dot16(a, b, dims):
    return lax.dot_general(a, b, dims, preferred_element_type=F32)


def split2(x):
    high = x.astype(BF16)
    low = (x - high.astype(F32)).astype(BF16)
    return high, low


def split3(x):
    high = x.astype(BF16)
    rest = x - high.astype(F32)
    mid = rest.astype(BF16)
    low = (rest - mid.astype(F32)).astype(BF16)
    return high, mid, low


def planes_kernel(x_ref, out_ref):
    ib = x_ref.shape[1]
    rows = x_ref.shape[3]
    flat = out_ref.reshape(rows * ib, out_ref.shape[2])
    for i in range(ib):
        pair = jnp.concatenate([x_ref[0, i], x_ref[1, i]], axis=0)
        flat[pl.ds(i, rows, stride=ib), :] = pair.T


def planes_first(field, group):
    species, cells, points, planes = field.shape
    ib = 8
    return pl.pallas_call(
        planes_kernel,
        grid=(cells // ib,),
        in_specs=[pl.BlockSpec((2, ib, points, planes), lambda g: (group, g, 0, 0))],
        out_specs=pl.BlockSpec((planes, ib, 2 * points), lambda g: (0, g, 0)),
        out_shape=jax.ShapeDtypeStruct((planes, cells, 2 * points), F32),
        compiler_params=pltpu.CompilerParams(vmem_limit_bytes=VMEM_LIMIT),
        name="planes_first",
    )(field)


def lower_blocks(n):
    return [(r, c) for r in range(n) for c in range(r + 1)]


def store_lower(out_ref, main, cross):
    n = main.shape[0] // 128
    for b, (r, c) in enumerate(lower_blocks(n)):
        rs, cs = slice(128 * r, 128 * r + 128), slice(128 * c, 128 * c + 128)
        out_ref[128 * b : 128 * b + 128, :] = main[rs, cs] + cross[rs, cs] + cross[cs, rs].T


def gram_first_kernel(steps, ya_ref, yb_ref, out_ref, main, cross):
    step = pl.program_id(0)
    parts = [
        ref[:, 0, 0, tau].reshape(main.shape[0], 128) for ref in (ya_ref, yb_ref) for tau in range(2)
    ]
    high, low = split2(jnp.concatenate(parts, axis=1))
    mixed = dot16(high, low, NT)
    full = dot16(high, high, NT)

    @pl.when(step == 0)
    def _():
        main[...] = full
        cross[...] = mixed

    @pl.when(step > 0)
    def _():
        main[...] += full
        cross[...] += mixed

    @pl.when(step == steps - 1)
    def _():
        store_lower(out_ref, main, cross)


def gram_first(ya, yb, wide, narrow):
    size = wide * ya.shape[1]
    count = size // 128
    rows = 128 * (count * (count + 1) // 2)
    shape = (wide, 1, narrow, 2) + ya.shape[1:]
    spec = pl.BlockSpec((wide, 1, 1, 2) + ya.shape[1:], lambda g: (0, 0, g, 0, 0, 0))
    return pl.pallas_call(
        functools.partial(gram_first_kernel, narrow),
        grid=(narrow,),
        in_specs=[spec, spec],
        out_specs=pl.BlockSpec((rows, 128), lambda g: (0, 0)),
        out_shape=jax.ShapeDtypeStruct((rows, 128), F32),
        scratch_shapes=[pltpu.VMEM((size, size), F32), pltpu.VMEM((size, size), F32)],
        compiler_params=pltpu.CompilerParams(vmem_limit_bytes=VMEM_LIMIT),
        name="gram_first",
    )(ya.reshape(shape), yb.reshape(shape))


def summed_everywhere(packed, devices):
    rows = packed.shape[0]
    pieces = packed.reshape(devices, 1, rows * 128 // devices)
    own = jnp.sum(lax.all_to_all(pieces, ALL, 0, 0, tiled=True), axis=0)
    copies = jnp.broadcast_to(own[None], pieces.shape)
    return lax.all_to_all(copies, ALL, 0, 0, tiled=True).reshape(rows, 128)


NB = 16


def inverse_factor(gram):
    size = gram.shape[0]
    row = lax.broadcasted_iota(jnp.int32, (size, size), 0)
    col = lax.broadcasted_iota(jnp.int32, (size, size), 1)
    work = jnp.concatenate([gram, jnp.where(row == col, 1.0, 0.0).astype(F32)], axis=1)
    lane_row = lax.broadcasted_iota(jnp.int32, (NB, size), 0)
    done = []
    for b in range(size // NB):
        panel = work[:NB]
        left = size - NB * b
        cols = [
            jnp.broadcast_to(panel[:, NB * b + j : NB * b + j + 1], (NB, size)) for j in range(NB)
        ]
        pivots = jnp.ones((NB, size), F32)
        for k in range(NB):
            pivot = jnp.broadcast_to(cols[k][k : k + 1], (NB, size))
            ratio = jnp.where(lane_row > k, cols[k] * (1.0 / pivot), 0.0)
            for j in range(k + 1, NB):
                cols[j] = cols[j] - ratio * jnp.broadcast_to(cols[j][k : k + 1], (NB, size))
            both = jnp.concatenate([ratio, ratio], axis=1)
            panel = panel - both * jnp.broadcast_to(panel[k : k + 1], panel.shape)
            pivots = jnp.where(lane_row == k, pivot, pivots)
        scale = 1.0 / jnp.sqrt(pivots)
        panel = panel * jnp.concatenate([scale, scale], axis=1)
        done.append(panel[:, size:])
        if left > NB:
            high, mid, low = split3(panel)
            lhs = jnp.concatenate([high, high, high, mid, mid, low], axis=0)[:, :size]
            rhs = jnp.concatenate([high, mid, low, high, mid, high], axis=0)
            update = dot16(lhs, rhs, TN)
            work = work[NB:] - update[NB * (b + 1) :]
    return jnp.concatenate(done, axis=0)


def orthonormal_rows(rows):
    return dot32(inverse_factor(dot32(rows, rows, NT)), rows, NN)


def start_kernel(start_ref, out_ref):
    out_ref[...] = orthonormal_rows(start_ref[...].T)


def start_rows(start):
    return pl.pallas_call(
        start_kernel,
        out_shape=jax.ShapeDtypeStruct(start.shape[::-1], F32),
        compiler_params=pltpu.CompilerParams(vmem_limit_bytes=VMEM_LIMIT),
        name="start_rows",
    )(start)


def basis_kernel(packed_ref, start_ref, rows_ref, basis_ref, gram):
    n = gram.shape[0] // 128
    for b, (r, c) in enumerate(lower_blocks(n)):
        block = packed_ref[128 * b : 128 * b + 128, :]
        gram[128 * r : 128 * r + 128, 128 * c : 128 * c + 128] = block
        if r != c:
            gram[128 * c : 128 * c + 128, 128 * r : 128 * r + 128] = block.T

    def sweep(_, rows):
        return orthonormal_rows(dot32(rows, gram[...], NN))

    rows = lax.fori_loop(0, ITERS, sweep, start_ref[...])
    rows_ref[...] = rows
    basis_ref[...] = rows.T


def basis_rows(packed, start):
    rank, size = start.shape
    return pl.pallas_call(
        basis_kernel,
        out_shape=(
            jax.ShapeDtypeStruct((rank, size), F32),
            jax.ShapeDtypeStruct((size, rank), F32),
        ),
        scratch_shapes=[pltpu.VMEM((size, size), F32)],
        compiler_params=pltpu.CompilerParams(vmem_limit_bytes=VMEM_LIMIT),
        name="basis_rows",
    )(packed, start)


def reduce_kernel(rows_ref, ya_ref, yb_ref, red_ref, out_ref, main, cross):
    step = pl.program_id(0)
    rank = rows_ref.shape[0]

    bh, bl = split2(rows_ref[...])
    both = jnp.concatenate([bh, bl], axis=0)
    lane = lax.broadcasted_iota(jnp.int32, (rank, 128), 1)

    def work(y_ref):
        narrow = y_ref.shape[2]
        for m in range(narrow // 2):
            parts = [
                y_ref[:, 0, 2 * m + h, 0].reshape(rows_ref.shape[1], 128) for h in range(2)
            ]
            yh, yl = split2(jnp.concatenate(parts, axis=1))
            wide = dot16(both, yh, NN)
            got = wide[:rank] + (wide[rank:] + dot16(bh, yl, NN))
            a, b = got[:, :128], got[:, 128:]
            first = jnp.where(lane < 64, a, pltpu.roll(b, 64, 1))
            second = jnp.where(lane < 64, pltpu.roll(a, 64, 1), b)
            red_ref[0, 0, 0, :, 128 * m : 128 * m + 128] = first
            red_ref[0, 0, 1, :, 128 * m : 128 * m + 128] = second

    @pl.when(step < 2)
    def _():
        work(ya_ref)

    @pl.when(step >= 2)
    def _():
        work(yb_ref)

    stacked = jnp.concatenate([red_ref[0, 0, 0], red_ref[0, 0, 1]], axis=0)
    high, low = split2(stacked)
    full = dot16(high, high, TN)
    mixed = dot16(high, low, TN)

    @pl.when(step == 0)
    def _():
        main[...] = full
        cross[...] = mixed

    @pl.when(step > 0)
    def _():
        main[...] += full
        cross[...] += mixed

    @pl.when(step == 3)
    def _():
        store_lower(out_ref, main, cross)


def reduce_first(rows, ya, yb, wide, narrow):
    rank, size = rows.shape
    points = narrow * 64
    count = points // 128
    packed = 128 * (count * (count + 1) // 2)
    shape = (wide, 1, narrow, 2) + ya.shape[1:]
    block = (wide, 1, narrow, 1) + ya.shape[1:]
    return pl.pallas_call(
        reduce_kernel,
        grid=(4,),
        in_specs=[
            pl.BlockSpec((rank, size), lambda g: (0, 0)),
            pl.BlockSpec(block, lambda g: (0, 0, 0, jnp.minimum(g, 1), 0, 0)),
            pl.BlockSpec(block, lambda g: (0, 0, 0, jnp.maximum(g, 2) - 2, 0, 0)),
        ],
        out_specs=(
            pl.BlockSpec((1, 1, 2, rank, points), lambda g: (g // 2, g % 2, 0, 0, 0)),
            pl.BlockSpec((packed, 128), lambda g: (0, 0)),
        ),
        out_shape=(
            jax.ShapeDtypeStruct((2, 2, 2, rank, points), F32),
            jax.ShapeDtypeStruct((packed, 128), F32),
        ),
        scratch_shapes=[pltpu.VMEM((points, points), F32), pltpu.VMEM((points, points), F32)],
        compiler_params=pltpu.CompilerParams(vmem_limit_bytes=VMEM_LIMIT),
        name="reduce_first",
    )(rows, ya.reshape(shape), yb.reshape(shape))


def core_kernel(rows_ref, red_ref, out_ref):
    rank = rows_ref.shape[0]
    bh, bl = split2(rows_ref[...])
    both = jnp.concatenate([bh, bl], axis=0)
    for s in range(2):
        rh, rl = split2(red_ref[0, 0, s])
        wide = dot16(rh, both, NT)
        got = wide[:, :rank] + (wide[:, rank:] + dot16(rl, bh, NT))
        out_ref[:, 0, s] = got.reshape(out_ref.shape[0], got.shape[0] // out_ref.shape[0], rank)


def core_blocks(rows, red, narrow):
    rank, points = rows.shape
    per = red.shape[3] // narrow
    return pl.pallas_call(
        core_kernel,
        grid=(4,),
        in_specs=[
            pl.BlockSpec((rank, points), lambda g: (0, 0)),
            pl.BlockSpec((1, 1, 2, red.shape[3], points), lambda g: (g // 2, g % 2, 0, 0, 0)),
        ],
        out_specs=pl.BlockSpec((narrow, 1, 2, per, rank), lambda g: (0, g % 2, g // 2, 0, 0)),
        out_shape=jax.ShapeDtypeStruct((narrow, 2, 4, per, rank), F32),
        compiler_params=pltpu.CompilerParams(vmem_limit_bytes=VMEM_LIMIT),
        name="core_blocks",
    )(rows, red)


def local(field, start_first, start_second):
    wide, narrow = lax.axis_size("wide"), lax.axis_size("narrow")
    ya = lax.all_to_all(planes_first(field, 0), ALL, 0, 0, tiled=True)
    yb = lax.all_to_all(planes_first(field, 1), ALL, 0, 0, tiled=True)
    rows_first = start_rows(start_first)
    rows_second = start_rows(start_second)
    packed = summed_everywhere(gram_first(ya, yb, wide, narrow), wide * narrow)
    rows_first, basis_first = basis_rows(packed, rows_first)
    red, packed = reduce_first(rows_first, ya, yb, wide, narrow)
    packed = summed_everywhere(packed, wide * narrow)
    rows_second, basis_second = basis_rows(packed, rows_second)
    core = core_blocks(rows_second, red, narrow)
    core = lax.all_to_all(core, "narrow", 0, 0, tiled=True)
    core = core.reshape(2 * narrow, *core.shape[2:])
    return (core, basis_first, basis_second)


def solution(mesh):
    placed = (P(None, "wide", "narrow", None), P(), P())
    return jax.shard_map(
        local,
        mesh=mesh,
        in_specs=placed,
        out_specs=(P("wide", None, "narrow", None), P(), P()),
        check_vma=False,
    )
```

time: 865 us -> 285 us (0.33)
  other arithmetic: 389 us -> 0.83 us
  local copies, waits for them, and re-layouts: 185 us -> 4.91 us
  Pallas kernels: 0 us -> 81.6 us
  matrix products: 76.9 us -> 0 us
  blocking collectives: 64.5 us -> 110 us
  waiting for transfers between devices: 94.5 us -> 61.4 us
  starting transfers between devices: 41.1 us -> 22.6 us
    another operation x69 -> x0, other arithmetic: 349 us -> none  [the longest x24 102 us: orthonormal(): lower_factor = jnp.linalg.cholesky(gram_matrix)]
    pallas_call x0 -> x9, Pallas kernels: none -> 81.6 us  [the longest x2 34.1 us: basis_rows(): pl.pallas_call(basis_kernel, out_shape=(jax.ShapeDtypeStruct((rank, size)...]
    unnamed x29 -> x5, local copies, waits for them, and re-layouts: 75.5 us -> 2.51 us
    dot_general x25 -> x0, matrix products: 59.2 us -> none  [the longest x2 18.9 us: first_local(): jnp.einsum('siq,sjq->sij', merged, merged, precision=lax.Precision.HIGHEST)]
    all_to_all x6 -> x0, local copies, waits for them, and re-layouts: 48.7 us -> none  [the longest x3 33.1 us: items_in_groups(): lax.all_to_all(group, axis, split_axis=split_dim, concat_axis=concat_dim,...]
    all_to_all x3 -> x4, blocking collectives: 64.5 us -> 110 us  [the longest x1 57.9 us: local(): yb = lax.all_to_all(planes_first(field, 1), ALL, 0, 0, tiled=True)]
    all_to_all x3 -> x0, other arithmetic: 34.6 us -> none  [the longest x2 27.4 us: items_in_groups(): lax.all_to_all(group, axis, split_axis=split_dim, concat_axis=concat_dim,...]
    all_to_all x6 -> x3, waiting for transfers between devices: 94.5 us -> 61.4 us  [the longest x1 45.1 us: local(): ya = lax.all_to_all(planes_first(field, 0), ALL, 0, 0, tiled=True)]
  transfers between devices with their start and end apart: 6 -> 3, of which waited for: 4 -> 3; matrix products, arithmetic and copies ran while one was open for 15% -> 0% of each run, Pallas kernels for 0% -> 6%
where the time goes in v1:
time: 285 us; the launch traced here: 282 us
  blocking collectives  110 us (39%)
  Pallas kernels  81.6 us (29%)
  waiting for transfers between devices  61.4 us (22%)
  starting transfers between devices  22.6 us (8%)
  local copies, waits for them, and re-layouts  4.91 us (2%)
    all_to_all x1, blocking collectives, local(): yb = lax.all_to_all(planes_first(field, 1), ALL, 0, 0, tiled=True)  57.9 us
    all_to_all x1, waiting for transfers between devices, local(): ya = lax.all_to_all(planes_first(field, 0), ALL, 0, 0, tiled=True)  45.1 us
    all_to_all x2, blocking collectives, summed_everywhere(): own = jnp.sum(lax.all_to_all(pieces, ALL, 0, 0, tiled=True), axis=0)  40.9 us
    pallas_call x2, Pallas kernels, basis_rows(): pl.pallas_call(basis_kernel, out_shape=(jax.ShapeDtypeStruct((rank, size)...  34.1 us
    all_to_all x2, waiting for transfers between devices, summed_everywhere(): return lax.all_to_all(copies, ALL, 0, 0, tiled=True).reshape(rows, 128)  16.3 us
    pallas_call x2, Pallas kernels, start_rows(): pl.pallas_call(start_kernel, out_shape=jax.ShapeDtypeStruct(start.shape[:...  12.2 us
    all_to_all x1, starting transfers between devices, local(): ya = lax.all_to_all(planes_first(field, 0), ALL, 0, 0, tiled=True)  11.9 us
    all_to_all x1, blocking collectives, local(): core = lax.all_to_all(core, 'narrow', 0, 0, tiled=True)  11.7 us
  transfers between devices with their start and end apart: 3, of which 3 were waited for; matrix products, arithmetic and copies ran while one was open for 0% of the time, Pallas kernels for 6%

profile of v1, /device:TPU:1, one launch (start us, length us, event | category | flops | bytes accessed | tf_op | source)
XLA Modules:
  0.0 282.5 jit_solution(7374112830808095529)
XLA Ops:
  0.6 5.4 %planes_first.2 = f32[256,32,128]{2,1,0:T(8,128)} custom-call(f32[4,32,64,256]{3,2,1,0:T(8,128)} %x_ref.3), custom_call_target="tpu_custom_call" | custom-call | tf_op jit(solution)/shard_map/planes_first/pallas_call | solution.py:55
  6.0 11.9 %all-to-all-start = ((f32[256,32,128]{2,1,0:T(8,128)}), f32[256,32,128]{2,1,0:T(8,128)}, u32[]{:S(2)}, u32[]{:S(2)}) async-start(f32[256,32,128]{2,1,0:T(8,128)} %planes_first.2), calls=%async_computation | async-start | bytes 8388608 | tf_op jit(solution)/shard_map/all_to_all | solution.py:321
  18.0 5.4 %planes_first.3 = f32[256,32,128]{2,1,0:T(8,128)} custom-call(f32[4,32,64,256]{3,2,1,0:T(8,128)} %x_ref.3), custom_call_target="tpu_custom_call" | custom-call | tf_op jit(solution)/shard_map/planes_first/pallas_call | solution.py:55
  23.3 45.1 %all-to-all-done = f32[256,32,128]{2,1,0:T(8,128)} async-done(((f32[256,32,128]{2,1,0:T(8,128)}), f32[256,32,128]{2,1,0:T(8,128)}, u32[]{:S(2)}, u32[]{:S(2)}) %all-to-all-start) | async-done | bytes 4194336 | tf_op jit(solution)/shard_map/all_to_all | solution.py:321
  68.4 57.9 %all_to_all.35 = f32[256,32,128]{2,1,0:T(8,128)} all-to-all(f32[256,32,128]{2,1,0:T(8,128)} %planes_first.3), channel_id=1, replica_groups=mesh['wide'=16,'narrow'=8] {'wide','narrow'}, dimensions={0} | all-to-all | bytes 8388608 | tf_op jit(solution)/shard_map/all_to_all | solution.py:322
  126.3 10.8 %gram_first.1 = f32[1280,128]{1,0:T(8,128)} custom-call(f32[16,1,8,2,32,128]{5,4,3,2,1,0:T(8,128)} %bitcast.ya_ref, f32[16,1,8,2,32,128]{5,4,3,2,1,0:T(8,128)} %bitcast.7), custom_call_target="tpu_custom_call" | custom-call | tf_op jit(solution)/shard_map/gram_first/pallas_call | solution.py:107
  137.1 21.2 %all_to_all.36 = f32[128,1,1280]{2,1,0:T(1,128)S(1)} all-to-all(f32[128,1,1280]{2,1,0:T(1,128)} %bitcast.9), channel_id=1, replica_groups=mesh['wide'=16,'narrow'=8] {'wide','narrow'}, dimensions={0} | all-to-all | bytes 1310720 | tf_op jit(solution)/shard_map/all_to_all | solution.py:122
  158.4 0.4 reduce_sum.18
  158.8 1.2 broadcast_in_dim.4
  160.0 5.4 %all-to-all-start.3 = ((f32[128,1,1280]{2,1,0:T(1,128)}), f32[128,1,1280]{2,1,0:T(1,128)S(1)}, u32[]{:S(2)}, u32[]{:S(2)}) async-start(f32[128,1,1280]{2,1,0:T(1,128)} %broadcast_in_dim.4), calls=%async_computation.3 | async-start | bytes 1310720 | tf_op jit(solution)/shard_map/all_to_all | solution.py:124
  165.4 6.1 %start_rows.2.start_ref = f32[128,512]{1,0:T(8,128)} custom-call(f32[512,128]{1,0:T(8,128)} %start_ref.2), custom_call_target="tpu_custom_call" | custom-call | tf_op jit(solution)/shard_map/start_rows/pallas_call | solution.py:173
  171.4 8.1 %all-to-all-done.3 = f32[128,1,1280]{2,1,0:T(1,128)S(1)} async-done(((f32[128,1,1280]{2,1,0:T(1,128)}), f32[128,1,1280]{2,1,0:T(1,128)S(1)}, u32[]{:S(2)}, u32[]{:S(2)}) %all-to-all-start.3) | async-done | bytes 655392 | tf_op jit(solution)/shard_map/all_to_all | solution.py:124
  179.6 0.0 copy-start
  179.6 0.9 copy-done
  180.5 17.0 %basis_rows.2 = (f32[128,512]{1,0:T(8,128)}, f32[512,128]{1,0:T(8,128)}) custom-call(f32[1280,128]{1,0:T(8,128)} %bitcast.10, f32[128,512]{1,0:T(8,128)} %start_rows.2.start_ref), custom_call_target="tpu_custom_call" | custom-call | tf_op jit(solution)/shard_map/basis_rows/pallas_call | solution.py:199
  197.5 9.5 %reduce_first.1 = (f32[2,2,2,128,512]{4,3,2,1,0:T(8,128)}, f32[1280,128]{1,0:T(8,128)}) custom-call(f32[128,512]{1,0:T(8,128)} %get-tuple-element.9.rows_ref, f32[16,1,8,2,32,128]{5,4,3,2,1,0:T(8,128)} %bitcast.ya_ref, f32[16,1,8,2,32,128]{5,4,3,2,1,0:T(8,128)} %bitcast.8), custom_call_target="tpu_custom_call" | custom-call | tf_op jit(solution)/shard_map/reduce_first/pallas_call | solution.py:269
  207.0 19.6 %all_to_all.37 = f32[128,1,1280]{2,1,0:T(1,128)S(1)} all-to-all(f32[128,1,1280]{2,1,0:T(1,128)} %bitcast.13), channel_id=1, replica_groups=mesh['wide'=16,'narrow'=8] {'wide','narrow'}, dimensions={0} | all-to-all | bytes 1310720 | tf_op jit(solution)/shard_map/all_to_all | solution.py:122
  226.7 0.4 reduce_sum.19
  227.1 1.2 broadcast_in_dim.5
  228.3 5.4 %all-to-all-start.5 = ((f32[128,1,1280]{2,1,0:T(1,128)}), f32[128,1,1280]{2,1,0:T(1,128)S(1)}, u32[]{:S(2)}, u32[]{:S(2)}) async-start(f32[128,1,1280]{2,1,0:T(1,128)} %broadcast_in_dim.5), calls=%async_computation.5 | async-start | bytes 1310720 | tf_op jit(solution)/shard_map/all_to_all | solution.py:124
  233.6 6.1 %start_rows.3.start_ref = f32[128,512]{1,0:T(8,128)} custom-call(f32[512,128]{1,0:T(8,128)} %start_ref.3), custom_call_target="tpu_custom_call" | custom-call | tf_op jit(solution)/shard_map/start_rows/pallas_call | solution.py:173
  239.7 8.1 %all-to-all-done.5 = f32[128,1,1280]{2,1,0:T(1,128)S(1)} async-done(((f32[128,1,1280]{2,1,0:T(1,128)}), f32[128,1,1280]{2,1,0:T(1,128)S(1)}, u32[]{:S(2)}, u32[]{:S(2)}) %all-to-all-start.5) | async-done | bytes 655392 | tf_op jit(solution)/shard_map/all_to_all | solution.py:124
  247.9 0.0 copy-start.1
  247.9 0.8 copy-done.1
  248.7 17.0 %basis_rows.3 = (f32[128,512]{1,0:T(8,128)}, f32[512,128]{1,0:T(8,128)}) custom-call(f32[1280,128]{1,0:T(8,128)} %bitcast.11, f32[128,512]{1,0:T(8,128)} %start_rows.3.start_ref), custom_call_target="tpu_custom_call" | custom-call | tf_op jit(solution)/shard_map/basis_rows/pallas_call | solution.py:199
  265.7 4.3 %core_blocks.1 = f32[8,2,4,16,128]{4,3,2,1,0:T(8,128)} custom-call(f32[128,512]{1,0:T(8,128)} %get-tuple-element.11.rows_ref, f32[2,2,2,128,512]{4,3,2,1,0:T(8,128)} %get-tuple-element.12.red_ref), custom_call_target="tpu_custom_call" | custom-call | tf_op jit(solution)/shard_map/core_blocks/pallas_call | solution.py:305
  270.0 11.7 %all_to_all.38 = f32[8,2,4,16,128]{4,3,2,1,0:T(8,128)S(1)} all-to-all(f32[8,2,4,16,128]{4,3,2,1,0:T(8,128)} %core_blocks.1), channel_id=1, replica_groups=mesh['wide'=16,'narrow'=8] {'narrow'}, dimensions={0} | all-to-all | bytes 1048576 | tf_op jit(solution)/shard_map/all_to_all | solution.py:331
  281.7 0.8 copy.9
Async XLA Ops:
  6.0 62.4 %all-to-all-start = ((f32[256,32,128]{2,1,0:T(8,128)}), f32[256,32,128]{2,1,0:T(8,128)}, u32[]{:S(2)}, u32[]{:S(2)}) async-start(f32[256,32,128]{2,1,0:T(8,128)} %planes_first.2), calls=%async_computation | async-start | bytes 8388608 | tf_op jit(solution)/shard_map/all_to_all | solution.py:321
  160.0 19.6 %all-to-all-start.3 = ((f32[128,1,1280]{2,1,0:T(1,128)}), f32[128,1,1280]{2,1,0:T(1,128)S(1)}, u32[]{:S(2)}, u32[]{:S(2)}) async-start(f32[128,1,1280]{2,1,0:T(1,128)} %broadcast_in_dim.4), calls=%async_computation.3 | async-start | bytes 1310720 | tf_op jit(solution)/shard_map/all_to_all | solution.py:124
  179.6 0.9 copy-start
  228.3 19.6 %all-to-all-start.5 = ((f32[128,1,1280]{2,1,0:T(1,128)}), f32[128,1,1280]{2,1,0:T(1,128)S(1)}, u32[]{:S(2)}, u32[]{:S(2)}) async-start(f32[128,1,1280]{2,1,0:T(1,128)} %broadcast_in_dim.5), calls=%async_computation.5 | async-start | bytes 1310720 | tf_op jit(solution)/shard_map/all_to_all | solution.py:124
  247.9 0.8 copy-start.1
